TPU v7x, 128 devices: a whole 4x4x4 slice. The times are simulated.
128 devices in a mesh: gx: 8 (over x, core), gy: 16 (over z, y).
Axes of the slice: x: 4, y: 4, z: 4, core: 2. Of those that a mesh axis runs over, the one named last changes fastest.
Arguments:
- parent_fields: float32 [5, 4, 384, 6144], P(None, None, 'gx', 'gy'), may hold values from -6 to 6
- parent_velocity: float32 [2, 4, 384, 6144], P(None, None, 'gx', 'gy'), may hold values from -0.3 to 0.3
- parent_mixing: float32 [4, 384, 6144], P(None, 'gx', 'gy'), may hold values from 0.01 to 0.1
- nest_fields: float32 [5, 4, 384, 6144], P(None, None, 'gx', 'gy'), may hold values from -6 to 6
- nest_velocity: float32 [2, 4, 384, 6144], P(None, None, 'gx', 'gy'), may hold values from -0.3 to 0.3
- nest_mixing: float32 [4, 384, 6144], P(None, 'gx', 'gy'), may hold values from 0.01 to 0.1
- nest_anchor: int32 [2], replicated, may hold values from 1 to 3327, as said below
Outputs:
- parent_result: float32 [5, 4, 384, 6144], P(None, None, 'gx', 'gy')
- nest_result: float32 [5, 4, 384, 6144], P(None, None, 'gx', 'gy')
Inputs may be any that keep to these rules, and one draw needn't show every extreme that they name: `nest_anchor`: the row anchor is 1 to 254; the column anchor is 3073 to 3327, so the nest with a rim of one parent cell lies inside the parent grid.
All inputs are finite; a program needn't handle non-finite values.
Results may differ from a plain program's by a relative error of at most 0.00002.
Values sent between devices are 32-bit elements; how exact they have to be, the bound alone decides.
A program may use at most 192 MiB of HBM per device.

v0:
```python
import jax
import jax.numpy as jnp
from jax import lax
from jax.sharding import PartitionSpec as P

SUBSTEPS = 3
third = 1.0 / 3.0
two_thirds = 2.0 / 3.0
nudge_floor = 0.1
relax_width = 4.0


def shift_pairs(count, step):
    return [(i, i + step) for i in range(count) if 0 <= i + step < count]


def neighbours(cells):
    rows = lax.axis_size("gx")
    cols = lax.axis_size("gy")
    western = lax.ppermute(cells[:, :, -1:, :], "gx", shift_pairs(rows, 1))
    eastern = lax.ppermute(cells[:, :, :1, :], "gx", shift_pairs(rows, -1))
    southern = lax.ppermute(cells[:, :, :, -1:], "gy", shift_pairs(cols, 1))
    northern = lax.ppermute(cells[:, :, :, :1], "gy", shift_pairs(cols, -1))
    return (western, eastern, southern, northern)


def update(values, halo, velocity, mixing):
    west_row, east_row, south_col, north_col = halo
    western = jnp.concatenate([west_row, values[:, :, :-1, :]], axis=2)
    eastern = jnp.concatenate([values[:, :, 1:, :], east_row], axis=2)
    southern = jnp.concatenate([south_col, values[:, :, :, :-1]], axis=3)
    northern = jnp.concatenate([values[:, :, :, 1:], north_col], axis=3)
    along_rows = velocity[0]
    along_columns = velocity[1]
    upwind = (
        jnp.maximum(along_rows, 0.0) * (values - western)
        + jnp.minimum(along_rows, 0.0) * (eastern - values)
        + jnp.maximum(along_columns, 0.0) * (values - southern)
        + jnp.minimum(along_columns, 0.0) * (northern - values)
    )
    return values - upwind + mixing * (eastern + western + northern + southern - 4.0 * values)


def refine_rows(block):
    lower = block[:, :, :-2]
    centre = block[:, :, 1:-1]
    upper = block[:, :, 2:]
    stacked = jnp.stack(
        (third * lower + two_thirds * centre, centre, two_thirds * centre + third * upper), axis=3
    )
    extent = centre.shape
    return stacked.reshape(extent[0], extent[1], 3 * extent[2], extent[3])


def refine_columns(block):
    lower = block[:, :, :, :-2]
    centre = block[:, :, :, 1:-1]
    upper = block[:, :, :, 2:]
    stacked = jnp.stack(
        (third * lower + two_thirds * centre, centre, two_thirds * centre + third * upper), axis=4
    )
    extent = centre.shape
    return stacked.reshape(extent[0], extent[1], extent[2], 3 * extent[3])


def grouping(count):
    rows = jnp.arange(count, dtype=jnp.int32)[:, None] // 3
    return (rows == jnp.arange(count // 3, dtype=jnp.int32)[None, :]).astype(jnp.float32)


def block_mean(state):
    extent = state.shape
    exact = lax.Precision.HIGHEST
    across = jnp.einsum("flrc,cb->flrb", state, grouping(extent[3]), precision=exact)
    down = jnp.einsum("ra,flrb->flab", grouping(extent[2]), across, precision=exact)
    return down / 9.0


def relax_weight(row_global, column_global, total_rows, total_columns):
    row_distance = jnp.minimum(row_global, total_rows - 1 - row_global)
    column_distance = jnp.minimum(column_global, total_columns - 1 - column_global)
    distance = jnp.minimum(row_distance[:, None], column_distance[None, :]).astype(jnp.float32)
    return nudge_floor + (1.0 - nudge_floor) * jnp.exp(-distance / relax_width)


def within(positions, limit):
    return (positions >= 0) & (positions < limit)


def column_pairs(count, base, ratio, k, extra):
    pairs = []
    for m in range(count):
        j = ratio * m + k
        p = base + m + extra
        if j < count and p < count:
            pairs.append((p, j))
    return pairs


def per_device(
    parent_fields,
    parent_velocity,
    parent_mixing,
    nest_fields,
    nest_velocity,
    nest_mixing,
    nest_anchor,
):
    row_rank = lax.axis_index("gx")
    column_rank = lax.axis_index("gy")
    row_devices = lax.axis_size("gx")
    column_devices = lax.axis_size("gy")
    parent_rows = parent_fields.shape[2]
    parent_columns = parent_fields.shape[3]
    nest_rows = nest_fields.shape[2]
    nest_columns = nest_fields.shape[3]
    span_rows = nest_rows // 3
    span_columns = nest_columns // 3
    ratio = parent_columns // span_columns
    base = column_devices // 2
    base_column = base * parent_columns
    relay_rows = span_rows + 2
    relay_columns = span_columns + 2
    row_anchor = nest_anchor[0]
    column_anchor = nest_anchor[1]
    offset = column_anchor - 1 - base_column
    parent_next = update(parent_fields, neighbours(parent_fields), parent_velocity, parent_mixing)
    margin = parent_columns - span_columns
    wide = jnp.pad(parent_next, ((0, 0), (0, 0), (0, 0), (margin, margin)))
    relay_cols = None
    for k in range(ratio):
        for extra in (0, 1):
            if extra == 1 and k == 0:
                continue
            start = margin + span_columns * k + offset - extra * parent_columns
            piece = lax.dynamic_slice_in_dim(wide, start, relay_columns, axis=3)
            moved = lax.ppermute(piece, "gy", column_pairs(column_devices, base, ratio, k, extra))
            relay_cols = moved if relay_cols is None else relay_cols + moved
    padded = jnp.pad(relay_cols, ((0, 0), (0, 0), (relay_rows, relay_rows), (0, 0)))
    slots = []
    for target in range(row_devices):
        first = row_anchor - 1 + span_rows * target - parent_rows * row_rank
        first = jnp.clip(first, -relay_rows, parent_rows) + relay_rows
        slots.append(lax.dynamic_slice_in_dim(padded, first, relay_rows, axis=2))
    stacked = jnp.stack(slots, axis=0)
    received = lax.all_to_all(stacked, "gx", split_axis=0, concat_axis=0, tiled=True)
    relay = jnp.sum(received, axis=0)
    forcing = refine_columns(refine_rows(relay))
    row_global = row_rank * nest_rows + jnp.arange(nest_rows, dtype=jnp.int32)
    column_global = column_rank * nest_columns + jnp.arange(nest_columns, dtype=jnp.int32)
    weight = relax_weight(
        row_global, column_global, row_devices * nest_rows, column_devices * nest_columns
    )
    state = nest_fields
    for substep in range(SUBSTEPS):
        moved = update(state, neighbours(state), nest_velocity, nest_mixing)
        state = moved + weight * (forcing - moved)
    coarse = block_mean(state)
    gathered = lax.all_gather(coarse, "gx", axis=2, tiled=True)
    total_span = row_devices * span_rows
    gathered = jnp.pad(gathered, ((0, 0), (0, 0), (parent_rows, parent_rows), (0, 0)))
    first = jnp.clip(parent_rows * row_rank - row_anchor, -parent_rows, total_span)
    strip = lax.dynamic_slice_in_dim(gathered, first + parent_rows, parent_rows, axis=2)
    pieces = []
    for extra in (1, 0):
        for k in range(ratio):
            if extra == 1 and k == 0:
                continue
            pairs = [(j, p) for p, j in column_pairs(column_devices, base, ratio, k, extra)]
            pieces.append(lax.ppermute(strip, "gy", pairs))
    joined = jnp.concatenate(pieces, axis=3)
    start = (ratio - 1) * span_columns - 1 - offset
    fed_back = lax.dynamic_slice_in_dim(joined, start, parent_columns, axis=3)
    relative_rows = row_rank * parent_rows + jnp.arange(parent_rows, dtype=jnp.int32) - row_anchor
    relative_columns = (
        column_rank * parent_columns + jnp.arange(parent_columns, dtype=jnp.int32) - column_anchor
    )
    rows_valid = within(relative_rows, total_span)
    columns_valid = within(relative_columns, column_devices * span_columns)
    covered = rows_valid[:, None] & columns_valid[None, :]
    parent_result = jnp.where(covered, fed_back, parent_next)
    return (parent_result, state)


def solution(mesh):
    placed = (
        P(None, None, "gx", "gy"),
        P(None, None, "gx", "gy"),
        P(None, "gx", "gy"),
        P(None, None, "gx", "gy"),
        P(None, None, "gx", "gy"),
        P(None, "gx", "gy"),
        P(),
    )
    return jax.shard_map(
        per_device,
        mesh=mesh,
        in_specs=placed,
        out_specs=(P(None, None, "gx", "gy"), P(None, None, "gx", "gy")),
        check_vma=False,
    )
```

profile of v0, /device:TPU:73, one launch (start us, length us, event | category | flops | bytes accessed | tf_op | source)
XLA Modules:
  0.0 324.5 jit_solution(11071260043738988761)
XLA Ops:
  7.2 2.4 fusion.37
  11.7 3.2 collective-permute-start.6
  15.6 3.1 collective-permute-start.5
  18.7 3.0 collective-permute-start.4
  33.1 3.7 %multiply_add_fusion.3 = f32[5,4,48,384]{3,2,1,0:T(8,128)S(1)} fusion(f32[5,4,48,384]{3,2,1,0:T(8,128)S(1)} %copy-done, f32[5,4,48,1]{3,2,1,0:T(8,128)} %collective-permute-done.7, f32[5,4,48,383]{3,2,1,0:T(8,128)} %get-tuple-element.38, f32[5,4,48,383]{3,2,1,0:T(8,128)S(1)} %get-tuple-element.37, f32[5,4,48,1]{3,2,1,0:T(8,128)} %collective-permute-done.6, ...), kind=kLoop, calls=%fused_computation.35 | loop fusion | flops 8478720 | bytes 10321920 | tf_op jit(solution)/shard_map/add | solution.py:41
  36.8 2.9 pad_dynamic-slice_fusion.3
  39.8 3.3 %collective-permute-start.12 = (f32[5,4,48,130]{3,2,1,0:T(8,128)}, f32[5,4,48,130]{3,2,1,0:T(8,128)}, u32[]{:S(2)}, u32[]{:S(2)}) collective-permute-start(f32[5,4,48,130]{3,2,1,0:T(8,128)} %get-tuple-element.29), channel_id=1, source_target_pairs={{9,2},{10,5},{11,8},{12,11},{13,14},{25,18},{26,21},{27,24},{28,27... | collective-permute-start | bytes 1497608 | tf_op jit(solution)/shard_map/ppermute | solution.py:137
  43.0 2.2 collective-permute-start.11
  45.3 2.2 collective-permute-start.10
  49.8 2.3 collective-permute-start.9
  58.9 25.7 %collective-permute-done.12 = f32[5,4,48,130]{3,2,1,0:T(8,128)} collective-permute-done((f32[5,4,48,130]{3,2,1,0:T(8,128)}, f32[5,4,48,130]{3,2,1,0:T(8,128)}, u32[]{:S(2)}, u32[]{:S(2)}) %collective-permute-start.12) | collective-permute-done | bytes 499232 | tf_op jit(solution)/shard_map/ppermute | solution.py:137
  84.6 28.6 %collective-permute-start.3 = (f32[5,4,48,1]{3,2,1,0:T(8,128)}, f32[5,4,48,1]{3,2,1,0:T(8,128)}, u32[]{:S(2)}, u32[]{:S(2)}) collective-permute-start(f32[5,4,48,1]{3,2,1,0:T(8,128)} %get-tuple-element.23), channel_id=1, source_target_pairs={{1,0},{2,1},{3,2},{4,3},{5,4},{6,5},{7,6},{8,7},{9,8},{10,9},{11,1... | collective-permute-start | bytes 11528 | tf_op jit(solution)/shard_map/ppermute | solution.py:23
  115.1 2.7 collective-permute-start.1
  117.9 2.8 collective-permute-start
  120.7 2.8 add_add_fusion
  131.5 4.6 %all-to-all-start = ((f32[8,5,4,18,130]{4,2,3,1,0:T(4,128)}), f32[8,5,4,18,130]{4,2,3,1,0:T(4,128)}, u32[]{:S(2)}, u32[]{:S(2)}) async-start(f32[8,5,4,18,130]{4,2,3,1,0:T(4,128)} %bitcast_dynamic-update-slice_fusion), calls=%async_computation | async-start | bytes 5898240 | tf_op jit(solution)/shard_map/all_to_all | solution.py:146
  142.0 29.8 %all-to-all-done = f32[8,5,4,18,130]{4,2,3,1,0:T(4,128)} async-done(((f32[8,5,4,18,130]{4,2,3,1,0:T(4,128)}), f32[8,5,4,18,130]{4,2,3,1,0:T(4,128)}, u32[]{:S(2)}, u32[]{:S(2)}) %all-to-all-start) | async-done | bytes 1497632 | tf_op jit(solution)/shard_map/all_to_all | solution.py:146
  171.8 2.5 reduce_sum.9
  176.3 3.6 %copy.41 = f32[5,4,48,128,3]{2,1,4,3,0:T(4,128)} copy(f32[5,4,48,128,3]{3,1,2,0,4:T(4,128)S(1)} %pad_maximum_fusion.8) | data formatting | bytes 2949120 | tf_op jit(solution)/shard_map/stack | solution.py:59
  179.9 3.4 %copy.42 = f32[5,4,48,384]{3,2,1,0:T(8,128)S(1)} copy(f32[5,4,48,384]{2,1,3,0:T(4,128)} %bitcast.62) | data formatting | bytes 2949120 | tf_op jit(solution)/shard_map/reshape | solution.py:63
  183.3 4.1 %multiply_add_fusion.2 = f32[5,4,48,384]{3,2,1,0:T(8,128)S(1)} fusion(f32[5,4,48,384]{3,2,1,0:T(8,128)S(1)} %copy.42, f32[5,4,48,384]{3,2,1,0:T(8,128)S(1)} %copy-done.1, f32[5,4,48,1]{3,2,1,0:T(8,128)} %collective-permute-done.3, f32[5,4,48,383]{3,2,1,0:T(8,128)} %get-tuple-element.25, f32[5,4,48,383]{3,2,1,0:T(8,128)} %get-tuple-element.24, ...), kind=kLoop, calls=%fused_computation.34 | loop fusion | flops 9584640 | bytes 11870208 | tf_op jit(solution)/shard_map/add | solution.py:157
  188.2 3.6 %collective-permute-start.16 = (f32[5,4,48,1]{3,2,1,0:T(8,128)S(1)}, f32[5,4,48,1]{3,2,1,0:T(8,128)S(1)}, u32[]{:S(2)}, u32[]{:S(2)}) collective-permute-start(f32[5,4,48,1]{3,2,1,0:T(8,128)S(1)} %get-tuple-element.15), channel_id=1, source_target_pairs={{1,0},{2,1},{3,2},{4,3},{5,4},{6,5},{7,6},{8,7},{9,8},{10,9},{11,1... | collective-permute-start | bytes 11528 | tf_op jit(solution)/shard_map/ppermute | solution.py:23
  193.8 3.1 collective-permute-start.14
  196.9 2.6 collective-permute-start.13
  202.0 4.7 %collective-permute-done.15 = f32[5,4,48,1]{3,2,1,0:T(8,128)S(1)} collective-permute-done((f32[5,4,48,1]{3,2,1,0:T(8,128)S(1)}, f32[5,4,48,1]{3,2,1,0:T(8,128)S(1)}, u32[]{:S(2)}, u32[]{:S(2)}) %collective-permute-start.15) | collective-permute-done | bytes 3872 | tf_op jit(solution)/shard_map/ppermute | solution.py:22
  209.2 5.2 %collective-permute-start.20 = (f32[5,4,48,1]{3,2,1,0:T(8,128)S(1)}, f32[5,4,48,1]{3,2,1,0:T(8,128)S(1)}, u32[]{:S(2)}, u32[]{:S(2)}) collective-permute-start(f32[5,4,48,1]{3,2,1,0:T(8,128)S(1)} %get-tuple-element.7), channel_id=1, source_target_pairs={{1,0},{2,1},{3,2},{4,3},{5,4},{6,5},{7,6},{8,7},{9,8},{10,9},{11,1... | collective-permute-start | bytes 11528 | tf_op jit(solution)/shard_map/ppermute | solution.py:23
  216.4 4.3 %collective-permute-start.18 = (f32[5,4,1,384]{3,2,1,0:T(1,128)S(1)}, f32[5,4,1,384]{3,2,1,0:T(1,128)S(1)}, u32[]{:S(2)}, u32[]{:S(2)}) collective-permute-start(f32[5,4,1,384]{3,2,1,0:T(1,128)S(1)} %get-tuple-element.3), channel_id=1, source_target_pairs={{16,0},{32,16},{48,32},{64,48},{80,64},{96,80},{112,96},{17,1},{33... | collective-permute-start | bytes 92168 | tf_op jit(solution)/shard_map/ppermute | solution.py:21
  223.0 3.7 %collective-permute-done.19 = f32[5,4,48,1]{3,2,1,0:T(8,128)S(1)} collective-permute-done((f32[5,4,48,1]{3,2,1,0:T(8,128)S(1)}, f32[5,4,48,1]{3,2,1,0:T(8,128)S(1)}, u32[]{:S(2)}, u32[]{:S(2)}) %collective-permute-start.19) | collective-permute-done | bytes 3872 | tf_op jit(solution)/shard_map/ppermute | solution.py:22
  230.9 25.4 %all-gather.2.cloned.1.call-done = f32[5,4,128,128]{3,2,1,0:T(8,128)} async-done(((f32[5,4,16,128]{3,2,1,0:T(8,128)}), f32[5,4,128,128]{3,2,1,0:T(8,128)}) %all-gather.2.cloned.1.call-update) | async-done | bytes 1310736 | tf_op jit(solution)/shard_map/all_gather | solution.py:159
  260.5 5.3 %collective-permute-start.23 = (f32[5,4,48,128]{3,2,1,0:T(8,128)S(1)}, f32[5,4,48,128]{3,2,1,0:T(8,128)S(1)}, u32[]{:S(2)}, u32[]{:S(2)}) collective-permute-start(f32[5,4,48,128]{3,2,1,0:T(8,128)S(1)} %pad_dynamic-slice_fusion.13), channel_id=1, source_target_pairs={{0,8},{3,9},{6,10},{9,11},{12,12},{15,13},{16,24},{19,25},{22,26},... | collective-permute-start | bytes 1474568 | tf_op jit(solution)/shard_map/ppermute | solution.py:170
  269.1 35.8 %collective-permute-done.21 = f32[5,4,48,128]{3,2,1,0:T(8,128)S(1)} collective-permute-done((f32[5,4,48,128]{3,2,1,0:T(8,128)S(1)}, f32[5,4,48,128]{3,2,1,0:T(8,128)S(1)}, u32[]{:S(2)}, u32[]{:S(2)}) %collective-permute-start.21) | collective-permute-done | bytes 491552 | tf_op jit(solution)/shard_map/ppermute | solution.py:170
  305.1 10.8 %collective-permute-done.25 = f32[5,4,48,128]{3,2,1,0:T(8,128)S(1)} collective-permute-done((f32[5,4,48,128]{3,2,1,0:T(8,128)S(1)}, f32[5,4,48,128]{3,2,1,0:T(8,128)S(1)}, u32[]{:S(2)}, u32[]{:S(2)}) %collective-permute-start.25) | collective-permute-done | bytes 491552 | tf_op jit(solution)/shard_map/ppermute | solution.py:170
  (109 shorter events, 54.2 us)
Async XLA Ops:
  9.6 23.5 %collective-permute-start.7 = (f32[5,4,48,1]{3,2,1,0:T(8,128)}, f32[5,4,48,1]{3,2,1,0:T(8,128)}, u32[]{:S(2)}, u32[]{:S(2)}) collective-permute-start(f32[5,4,48,1]{3,2,1,0:T(8,128)} %get-tuple-element.36), channel_id=1, source_target_pairs={{1,0},{2,1},{3,2},{4,3},{5,4},{6,5},{7,6},{8,7},{9,8},{10,9},{11,1... | collective-permute-start | bytes 11528 | tf_op jit(solution)/shard_map/ppermute | solution.py:23
  11.7 21.4 %collective-permute-start.6 = (f32[5,4,48,1]{3,2,1,0:T(8,128)}, f32[5,4,48,1]{3,2,1,0:T(8,128)}, u32[]{:S(2)}, u32[]{:S(2)}) collective-permute-start(f32[5,4,48,1]{3,2,1,0:T(8,128)} %get-tuple-element.35), channel_id=1, source_target_pairs={{0,1},{1,2},{2,3},{3,4},{4,5},{5,6},{6,7},{7,8},{8,9},{9,10},{10,1... | collective-permute-start | bytes 11528 | tf_op jit(solution)/shard_map/ppermute | solution.py:22
  15.6 17.5 %collective-permute-start.5 = (f32[5,4,1,384]{3,2,1,0:T(1,128)}, f32[5,4,1,384]{3,2,1,0:T(1,128)}, u32[]{:S(2)}, u32[]{:S(2)}) collective-permute-start(f32[5,4,1,384]{3,2,1,0:T(1,128)} %get-tuple-element.32), channel_id=1, source_target_pairs={{16,0},{32,16},{48,32},{64,48},{80,64},{96,80},{112,96},{17,1},{33... | collective-permute-start | bytes 92168 | tf_op jit(solution)/shard_map/ppermute | solution.py:21
  18.7 14.4 %collective-permute-start.4 = (f32[5,4,1,384]{3,2,1,0:T(1,128)}, f32[5,4,1,384]{3,2,1,0:T(1,128)}, u32[]{:S(2)}, u32[]{:S(2)}) collective-permute-start(f32[5,4,1,384]{3,2,1,0:T(1,128)} %get-tuple-element.31), channel_id=1, source_target_pairs={{0,16},{16,32},{32,48},{48,64},{64,80},{80,96},{96,112},{1,17},{17... | collective-permute-start | bytes 92168 | tf_op jit(solution)/shard_map/ppermute | solution.py:20
  36.8 20.3 %copy-start.1 = (f32[5,4,48,384]{3,2,1,0:T(8,128)S(1)}, f32[5,4,48,384]{3,2,1,0:T(8,128)}, u32[]{:S(2)}) copy-start(f32[5,4,48,384]{3,2,1,0:T(8,128)} %param.10) | copy-start | bytes 4423684
  39.8 44.8 %collective-permute-start.12 = (f32[5,4,48,130]{3,2,1,0:T(8,128)}, f32[5,4,48,130]{3,2,1,0:T(8,128)}, u32[]{:S(2)}, u32[]{:S(2)}) collective-permute-start(f32[5,4,48,130]{3,2,1,0:T(8,128)} %get-tuple-element.29), channel_id=1, source_target_pairs={{9,2},{10,5},{11,8},{12,11},{13,14},{25,18},{26,21},{27,24},{28,27... | collective-permute-start | bytes 1497608 | tf_op jit(solution)/shard_map/ppermute | solution.py:137
  43.0 70.1 %collective-permute-start.11 = (f32[5,4,48,130]{3,2,1,0:T(8,128)}, f32[5,4,48,130]{3,2,1,0:T(8,128)}, u32[]{:S(2)}, u32[]{:S(2)}) collective-permute-start(f32[5,4,48,130]{3,2,1,0:T(8,128)} %get-tuple-element.28), channel_id=1, source_target_pairs={{8,2},{9,5},{10,8},{11,11},{12,14},{24,18},{25,21},{26,24},{27,27}... | collective-permute-start | bytes 1497608 | tf_op jit(solution)/shard_map/ppermute | solution.py:137
  45.3 69.8 %collective-permute-start.10 = (f32[5,4,48,130]{3,2,1,0:T(8,128)}, f32[5,4,48,130]{3,2,1,0:T(8,128)}, u32[]{:S(2)}, u32[]{:S(2)}) collective-permute-start(f32[5,4,48,130]{3,2,1,0:T(8,128)} %get-tuple-element.27), channel_id=1, source_target_pairs={{9,1},{10,4},{11,7},{12,10},{13,13},{25,17},{26,20},{27,23},{28,26... | collective-permute-start | bytes 1497608 | tf_op jit(solution)/shard_map/ppermute | solution.py:137
  47.5 70.3 %collective-permute-start.8 = (f32[5,4,48,130]{3,2,1,0:T(8,128)S(1)}, f32[5,4,48,130]{3,2,1,0:T(8,128)}, u32[]{:S(2)}, u32[]{:S(2)}) collective-permute-start(f32[5,4,48,130]{3,2,1,0:T(8,128)S(1)} %get-tuple-element.30), channel_id=1, source_target_pairs={{8,0},{9,3},{10,6},{11,9},{12,12},{13,15},{24,16},{25,19},{26,22},... | collective-permute-start | bytes 1497608 | tf_op jit(solution)/shard_map/ppermute | solution.py:137
  49.8 71.0 %collective-permute-start.9 = (f32[5,4,48,130]{3,2,1,0:T(8,128)S(1)}, f32[5,4,48,130]{3,2,1,0:T(8,128)}, u32[]{:S(2)}, u32[]{:S(2)}) collective-permute-start(f32[5,4,48,130]{3,2,1,0:T(8,128)S(1)} %get-tuple-element.26), channel_id=1, source_target_pairs={{8,1},{9,4},{10,7},{11,10},{12,13},{24,17},{25,20},{26,23},{27,26}... | collective-permute-start | bytes 1497608 | tf_op jit(solution)/shard_map/ppermute | solution.py:137
  84.6 98.7 %collective-permute-start.3 = (f32[5,4,48,1]{3,2,1,0:T(8,128)}, f32[5,4,48,1]{3,2,1,0:T(8,128)}, u32[]{:S(2)}, u32[]{:S(2)}) collective-permute-start(f32[5,4,48,1]{3,2,1,0:T(8,128)} %get-tuple-element.23), channel_id=1, source_target_pairs={{1,0},{2,1},{3,2},{4,3},{5,4},{6,5},{7,6},{8,7},{9,8},{10,9},{11,1... | collective-permute-start | bytes 11528 | tf_op jit(solution)/shard_map/ppermute | solution.py:23
  113.2 70.1 %collective-permute-start.2 = (f32[5,4,48,1]{3,2,1,0:T(8,128)}, f32[5,4,48,1]{3,2,1,0:T(8,128)}, u32[]{:S(2)}, u32[]{:S(2)}) collective-permute-start(f32[5,4,48,1]{3,2,1,0:T(8,128)} %get-tuple-element.22), channel_id=1, source_target_pairs={{0,1},{1,2},{2,3},{3,4},{4,5},{5,6},{6,7},{7,8},{8,9},{9,10},{10,1... | collective-permute-start | bytes 11528 | tf_op jit(solution)/shard_map/ppermute | solution.py:22
  115.1 68.2 %collective-permute-start.1 = (f32[5,4,1,384]{3,2,1,0:T(1,128)}, f32[5,4,1,384]{3,2,1,0:T(1,128)}, u32[]{:S(2)}, u32[]{:S(2)}) collective-permute-start(f32[5,4,1,384]{3,2,1,0:T(1,128)} %get-tuple-element.19), channel_id=1, source_target_pairs={{16,0},{32,16},{48,32},{64,48},{80,64},{96,80},{112,96},{17,1},{33... | collective-permute-start | bytes 92168 | tf_op jit(solution)/shard_map/ppermute | solution.py:21
  117.9 65.4 %collective-permute-start = (f32[5,4,1,384]{3,2,1,0:T(1,128)}, f32[5,4,1,384]{3,2,1,0:T(1,128)}, u32[]{:S(2)}, u32[]{:S(2)}) collective-permute-start(f32[5,4,1,384]{3,2,1,0:T(1,128)} %get-tuple-element.18), channel_id=1, source_target_pairs={{0,16},{16,32},{32,48},{48,64},{64,80},{80,96},{96,112},{1,17},{17... | collective-permute-start | bytes 92168 | tf_op jit(solution)/shard_map/ppermute | solution.py:20
  131.5 40.2 %all-to-all-start = ((f32[8,5,4,18,130]{4,2,3,1,0:T(4,128)}), f32[8,5,4,18,130]{4,2,3,1,0:T(4,128)}, u32[]{:S(2)}, u32[]{:S(2)}) async-start(f32[8,5,4,18,130]{4,2,3,1,0:T(4,128)} %bitcast_dynamic-update-slice_fusion), calls=%async_computation | async-start | bytes 5898240 | tf_op jit(solution)/shard_map/all_to_all | solution.py:146
  136.2 120.2 %all-gather.2.cloned.1.call-start = ((), (), s32[]{:S(2)}) async-start(), calls=%async_computation.1 | async-start | bytes 1474560 | tf_op jit(solution)/shard_map/all_gather | solution.py:159
  188.2 13.8 %collective-permute-start.16 = (f32[5,4,48,1]{3,2,1,0:T(8,128)S(1)}, f32[5,4,48,1]{3,2,1,0:T(8,128)S(1)}, u32[]{:S(2)}, u32[]{:S(2)}) collective-permute-start(f32[5,4,48,1]{3,2,1,0:T(8,128)S(1)} %get-tuple-element.15), channel_id=1, source_target_pairs={{1,0},{2,1},{3,2},{4,3},{5,4},{6,5},{7,6},{8,7},{9,8},{10,9},{11,1... | collective-permute-start | bytes 11528 | tf_op jit(solution)/shard_map/ppermute | solution.py:23
  191.9 14.8 %collective-permute-start.15 = (f32[5,4,48,1]{3,2,1,0:T(8,128)S(1)}, f32[5,4,48,1]{3,2,1,0:T(8,128)S(1)}, u32[]{:S(2)}, u32[]{:S(2)}) collective-permute-start(f32[5,4,48,1]{3,2,1,0:T(8,128)S(1)} %get-tuple-element.14), channel_id=1, source_target_pairs={{0,1},{1,2},{2,3},{3,4},{4,5},{5,6},{6,7},{7,8},{8,9},{9,10},{10,1... | collective-permute-start | bytes 11528 | tf_op jit(solution)/shard_map/ppermute | solution.py:22
  193.8 12.9 %collective-permute-start.14 = (f32[5,4,1,384]{3,2,1,0:T(1,128)S(1)}, f32[5,4,1,384]{3,2,1,0:T(1,128)S(1)}, u32[]{:S(2)}, u32[]{:S(2)}) collective-permute-start(f32[5,4,1,384]{3,2,1,0:T(1,128)S(1)} %get-tuple-element.11), channel_id=1, source_target_pairs={{16,0},{32,16},{48,32},{64,48},{80,64},{96,80},{112,96},{17,1},{33... | collective-permute-start | bytes 92168 | tf_op jit(solution)/shard_map/ppermute | solution.py:21
  196.9 9.8 %copy-start.5 = (f32[4,48,384]{2,1,0:T(8,128)S(1)}, f32[4,48,384]{2,1,0:T(8,128)}, u32[]{:S(2)}) copy-start(f32[4,48,384]{2,1,0:T(8,128)} %get-tuple-element.52) | copy-start | bytes 884740
  196.9 9.8 %collective-permute-start.13 = (f32[5,4,1,384]{3,2,1,0:T(1,128)S(1)}, f32[5,4,1,384]{3,2,1,0:T(1,128)S(1)}, u32[]{:S(2)}, u32[]{:S(2)}) collective-permute-start(f32[5,4,1,384]{3,2,1,0:T(1,128)S(1)} %get-tuple-element.10), channel_id=1, source_target_pairs={{0,16},{16,32},{32,48},{48,64},{64,80},{80,96},{96,112},{1,17},{17... | collective-permute-start | bytes 92168 | tf_op jit(solution)/shard_map/ppermute | solution.py:20
  209.2 13.7 %collective-permute-start.20 = (f32[5,4,48,1]{3,2,1,0:T(8,128)S(1)}, f32[5,4,48,1]{3,2,1,0:T(8,128)S(1)}, u32[]{:S(2)}, u32[]{:S(2)}) collective-permute-start(f32[5,4,48,1]{3,2,1,0:T(8,128)S(1)} %get-tuple-element.7), channel_id=1, source_target_pairs={{1,0},{2,1},{3,2},{4,3},{5,4},{6,5},{7,6},{8,7},{9,8},{10,9},{11,1... | collective-permute-start | bytes 11528 | tf_op jit(solution)/shard_map/ppermute | solution.py:23
  214.4 12.3 %collective-permute-start.19 = (f32[5,4,48,1]{3,2,1,0:T(8,128)S(1)}, f32[5,4,48,1]{3,2,1,0:T(8,128)S(1)}, u32[]{:S(2)}, u32[]{:S(2)}) collective-permute-start(f32[5,4,48,1]{3,2,1,0:T(8,128)S(1)} %get-tuple-element.6), channel_id=1, source_target_pairs={{0,1},{1,2},{2,3},{3,4},{4,5},{5,6},{6,7},{7,8},{8,9},{9,10},{10,1... | collective-permute-start | bytes 11528 | tf_op jit(solution)/shard_map/ppermute | solution.py:22
  216.4 10.3 %collective-permute-start.18 = (f32[5,4,1,384]{3,2,1,0:T(1,128)S(1)}, f32[5,4,1,384]{3,2,1,0:T(1,128)S(1)}, u32[]{:S(2)}, u32[]{:S(2)}) collective-permute-start(f32[5,4,1,384]{3,2,1,0:T(1,128)S(1)} %get-tuple-element.3), channel_id=1, source_target_pairs={{16,0},{32,16},{48,32},{64,48},{80,64},{96,80},{112,96},{17,1},{33... | collective-permute-start | bytes 92168 | tf_op jit(solution)/shard_map/ppermute | solution.py:21
  220.6 6.1 %collective-permute-start.17 = (f32[5,4,1,384]{3,2,1,0:T(1,128)S(1)}, f32[5,4,1,384]{3,2,1,0:T(1,128)S(1)}, u32[]{:S(2)}, u32[]{:S(2)}) collective-permute-start(f32[5,4,1,384]{3,2,1,0:T(1,128)S(1)} %get-tuple-element.2), channel_id=1, source_target_pairs={{0,16},{16,32},{32,48},{48,64},{64,80},{80,96},{96,112},{1,17},{17... | collective-permute-start | bytes 92168 | tf_op jit(solution)/shard_map/ppermute | solution.py:20
  228.4 28.8 %copy-start.4 = (f32[5,4,48,384]{3,2,1,0:T(8,128)}, f32[5,4,48,384]{3,2,1,0:T(8,128)S(1)}, u32[]{:S(2)}) copy-start(f32[5,4,48,384]{3,2,1,0:T(8,128)S(1)} %multiply_add_fusion) | copy-start | bytes 4423684
  257.3 47.6 %collective-permute-start.21 = (f32[5,4,48,128]{3,2,1,0:T(8,128)S(1)}, f32[5,4,48,128]{3,2,1,0:T(8,128)S(1)}, u32[]{:S(2)}, u32[]{:S(2)}) collective-permute-start(f32[5,4,48,128]{3,2,1,0:T(8,128)S(1)} %pad_dynamic-slice_fusion.13), channel_id=1, source_target_pairs={{1,9},{4,10},{7,11},{10,12},{13,13},{17,25},{20,26},{23,27},{26,28... | collective-permute-start | bytes 1474568 | tf_op jit(solution)/shard_map/ppermute | solution.py:170
  258.6 46.4 %collective-permute-start.22 = (f32[5,4,48,128]{3,2,1,0:T(8,128)S(1)}, f32[5,4,48,128]{3,2,1,0:T(8,128)S(1)}, u32[]{:S(2)}, u32[]{:S(2)}) collective-permute-start(f32[5,4,48,128]{3,2,1,0:T(8,128)S(1)} %pad_dynamic-slice_fusion.13), channel_id=1, source_target_pairs={{2,9},{5,10},{8,11},{11,12},{14,13},{18,25},{21,26},{24,27},{27,28... | collective-permute-start | bytes 1474568 | tf_op jit(solution)/shard_map/ppermute | solution.py:170
  260.5 44.5 %collective-permute-start.23 = (f32[5,4,48,128]{3,2,1,0:T(8,128)S(1)}, f32[5,4,48,128]{3,2,1,0:T(8,128)S(1)}, u32[]{:S(2)}, u32[]{:S(2)}) collective-permute-start(f32[5,4,48,128]{3,2,1,0:T(8,128)S(1)} %pad_dynamic-slice_fusion.13), channel_id=1, source_target_pairs={{0,8},{3,9},{6,10},{9,11},{12,12},{15,13},{16,24},{19,25},{22,26},... | collective-permute-start | bytes 1474568 | tf_op jit(solution)/shard_map/ppermute | solution.py:170
  266.4 38.6 %collective-permute-start.24 = (f32[5,4,48,128]{3,2,1,0:T(8,128)S(1)}, f32[5,4,48,128]{3,2,1,0:T(8,128)S(1)}, u32[]{:S(2)}, u32[]{:S(2)}) collective-permute-start(f32[5,4,48,128]{3,2,1,0:T(8,128)S(1)} %pad_dynamic-slice_fusion.13), channel_id=1, source_target_pairs={{1,8},{4,9},{7,10},{10,11},{13,12},{17,24},{20,25},{23,26},{26,27}... | collective-permute-start | bytes 1474568 | tf_op jit(solution)/shard_map/ppermute | solution.py:170
  267.8 48.1 %collective-permute-start.25 = (f32[5,4,48,128]{3,2,1,0:T(8,128)S(1)}, f32[5,4,48,128]{3,2,1,0:T(8,128)S(1)}, u32[]{:S(2)}, u32[]{:S(2)}) collective-permute-start(f32[5,4,48,128]{3,2,1,0:T(8,128)S(1)} %pad_dynamic-slice_fusion.13), channel_id=1, source_target_pairs={{2,8},{5,9},{8,10},{11,11},{14,12},{18,24},{21,25},{24,26},{27,27}... | collective-permute-start | bytes 1474568 | tf_op jit(solution)/shard_map/ppermute | solution.py:170
  305.0 11.0 %copy-start.3 = (f32[5,4,48,384]{3,2,1,0:T(8,128)S(1)}, f32[5,4,48,384]{3,2,1,0:T(8,128)}, u32[]{:S(2)}) copy-start(f32[5,4,48,384]{3,2,1,0:T(8,128)} %copy-done.2) | copy-start | bytes 4423684
  (8 other events, 48.3 us)
Sparse Core Ops, SparseCore 0:
  230.4 25.9 all-gather.1
where the time goes:
time: 326 us; the launch traced here: 324 us
  waiting for transfers between devices  138 us (42%)
  starting transfers between devices  99.6 us (31%)
  local copies, waits for them, and re-layouts  34.8 us (11%)
  between operations  26.7 us (8%)
  other arithmetic  23.4 us (7%)
    ppermute x5, waiting for transfers between devices, per_device(): pieces.append(lax.ppermute(strip, 'gy', pairs))  46.6 us
    ppermute x4, starting transfers between devices, neighbours(): northern = lax.ppermute(cells[:, :, :, :1], 'gy', shift_pairs(cols, -1))  39.5 us
    all_to_all x1, waiting for transfers between devices, per_device(): lax.all_to_all(stacked, 'gx', split_axis=0, concat_axis=0, tiled=True)  29.8 us
    ppermute x5, waiting for transfers between devices, per_device(): lax.ppermute(piece, 'gy', column_pairs(column_devices, base, ratio, k, ex...  25.7 us
    all_gather x1, waiting for transfers between devices, per_device(): gathered = lax.all_gather(coarse, 'gx', axis=2, tiled=True)  25.4 us
    ppermute x4, starting transfers between devices, neighbours(): eastern = lax.ppermute(cells[:, :, :1, :], 'gx', shift_pairs(rows, -1))  13.2 us
    ppermute x5, starting transfers between devices, per_device(): lax.ppermute(piece, 'gy', column_pairs(column_devices, base, ratio, k, ex...  12.3 us
    ppermute x4, starting transfers between devices, neighbours(): western = lax.ppermute(cells[:, :, -1:, :], 'gx', shift_pairs(rows, 1))  10.6 us
  transfers between devices with their start and end apart: 28, of which 8 were waited for; matrix products, arithmetic and copies ran while one was open for 12% of the time, Pallas kernels for 0%

commit v1 on v0

--- a/solution.py
+++ b/solution.py
@@ -156,7 +156,16 @@
         moved = update(state, neighbours(state), nest_velocity, nest_mixing)
         state = moved + weight * (forcing - moved)
     coarse = block_mean(state)
-    gathered = lax.all_gather(coarse, "gx", axis=2, tiled=True)
+    ways = lax.axis_size("gx")
+    up = [(d, (d + 1) % ways) for d in range(ways)]
+    down_2 = [(d, (d - 1) % ways) for d in range(ways)]
+    earlier, later = ([coarse], [coarse])
+    for _ in range(ways // 2):
+        earlier.append(lax.ppermute(earlier[-1], "gx", up))
+    for _ in range((ways - 1) // 2):
+        later.append(lax.ppermute(later[-1], "gx", down_2))
+    line = jnp.concatenate([*earlier[::-1], *later[1:]], axis=2)
+    gathered = jnp.roll(line, (lax.axis_index("gx") - ways // 2) * coarse.shape[2], axis=2)
     total_span = row_devices * span_rows
     gathered = jnp.pad(gathered, ((0, 0), (0, 0), (parent_rows, parent_rows), (0, 0)))
     first = jnp.clip(parent_rows * row_rank - row_anchor, -parent_rows, total_span)

time: 326 us -> 309 us (0.948)
  waiting for transfers between devices: 138 us -> 118 us
  starting transfers between devices: 99.6 us -> 117 us
  between operations: 26.7 us -> 13 us
    all_gather x1 -> x0, waiting for transfers between devices: 25.4 us -> none  [per_device(): gathered = lax.all_gather(coarse, 'gx', axis=2, tiled=True)]
    ppermute x0 -> x7, starting transfers between devices: none -> 16.5 us  [the longest x4 10 us: per_device(): earlier.append(lax.ppermute(earlier[-1], 'gx', up))]
    ppermute x0 -> x7, waiting for transfers between devices: none -> 5.78 us  [the longest x4 4.63 us: per_device(): earlier.append(lax.ppermute(earlier[-1], 'gx', up))]
    unnamed x35 -> x50, local copies, waits for them, and re-layouts: 6.43 us -> 6.69 us
  transfers between devices with their start and end apart: 28 -> 34, of which waited for: 8 -> 13; matrix products, arithmetic and copies ran while one was open for 12% -> 12% of each run, Pallas kernels for 0% -> 0%
where the time goes in v1:
time: 309 us; the launch traced here: 307 us
  waiting for transfers between devices  118 us (38%)
  starting transfers between devices  117 us (38%)
  local copies, waits for them, and re-layouts  34.3 us (11%)
  other arithmetic  23.3 us (8%)
  between operations  13 us (4%)
    ppermute x5, waiting for transfers between devices, per_device(): pieces.append(lax.ppermute(strip, 'gy', pairs))  45.7 us
    ppermute x4, starting transfers between devices, neighbours(): northern = lax.ppermute(cells[:, :, :, :1], 'gy', shift_pairs(cols, -1))  39.4 us
    all_to_all x1, waiting for transfers between devices, per_device(): lax.all_to_all(stacked, 'gx', split_axis=0, concat_axis=0, tiled=True)  29.8 us
    ppermute x5, waiting for transfers between devices, per_device(): lax.ppermute(piece, 'gy', column_pairs(column_devices, base, ratio, k, ex...  26.2 us
    ppermute x4, starting transfers between devices, neighbours(): eastern = lax.ppermute(cells[:, :, :1, :], 'gx', shift_pairs(rows, -1))  13.2 us
    ppermute x5, starting transfers between devices, per_device(): lax.ppermute(piece, 'gy', column_pairs(column_devices, base, ratio, k, ex...  12.3 us
    ppermute x5, starting transfers between devices, per_device(): pieces.append(lax.ppermute(strip, 'gy', pairs))  11.4 us
    ppermute x4, starting transfers between devices, neighbours(): western = lax.ppermute(cells[:, :, -1:, :], 'gx', shift_pairs(rows, 1))  10.6 us
  transfers between devices with their start and end apart: 34, of which 13 were waited for; matrix products, arithmetic and copies ran while one was open for 12% of the time, Pallas kernels for 0%

profile of v1, /device:TPU:73, one launch (start us, length us, event | category | flops | bytes accessed | tf_op | source)
XLA Modules:
  0.0 306.8 jit_solution(4806732629466987560)
XLA Ops:
  0.6 2.4 fusion.37
  5.1 3.2 %collective-permute-start.6 = (f32[5,4,48,1]{3,2,1,0:T(8,128)}, f32[5,4,48,1]{3,2,1,0:T(8,128)}, u32[]{:S(2)}, u32[]{:S(2)}) collective-permute-start(f32[5,4,48,1]{3,2,1,0:T(8,128)} %get-tuple-element.35), channel_id=1, source_target_pairs={{0,1},{1,2},{2,3},{3,4},{4,5},{5,6},{6,7},{7,8},{8,9},{9,10},{10,1... | collective-permute-start | bytes 11528 | tf_op jit(solution)/shard_map/ppermute | solution.py:22
  9.0 3.1 %collective-permute-start.5 = (f32[5,4,1,384]{3,2,1,0:T(1,128)}, f32[5,4,1,384]{3,2,1,0:T(1,128)}, u32[]{:S(2)}, u32[]{:S(2)}) collective-permute-start(f32[5,4,1,384]{3,2,1,0:T(1,128)} %get-tuple-element.32), channel_id=1, source_target_pairs={{16,0},{32,16},{48,32},{64,48},{80,64},{96,80},{112,96},{17,1},{33... | collective-permute-start | bytes 92168 | tf_op jit(solution)/shard_map/ppermute | solution.py:21
  12.1 3.0 collective-permute-start.4
  26.5 3.7 %multiply_add_fusion.3 = f32[5,4,48,384]{3,2,1,0:T(8,128)S(1)} fusion(f32[5,4,48,384]{3,2,1,0:T(8,128)S(1)} %copy-done, f32[5,4,48,1]{3,2,1,0:T(8,128)} %collective-permute-done.7, f32[5,4,48,383]{3,2,1,0:T(8,128)} %get-tuple-element.38, f32[5,4,48,383]{3,2,1,0:T(8,128)S(1)} %get-tuple-element.37, f32[5,4,48,1]{3,2,1,0:T(8,128)} %collective-permute-done.6, ...), kind=kLoop, calls=%fused_computation.35 | loop fusion | flops 8478720 | bytes 10321920 | tf_op jit(solution)/shard_map/add | solution.py:41
  30.2 2.9 pad_dynamic-slice_fusion.3
  33.2 3.3 %collective-permute-start.12 = (f32[5,4,48,130]{3,2,1,0:T(8,128)}, f32[5,4,48,130]{3,2,1,0:T(8,128)}, u32[]{:S(2)}, u32[]{:S(2)}) collective-permute-start(f32[5,4,48,130]{3,2,1,0:T(8,128)} %get-tuple-element.29), channel_id=1, source_target_pairs={{9,2},{10,5},{11,8},{12,11},{13,14},{25,18},{26,21},{27,24},{28,27... | collective-permute-start | bytes 1497608 | tf_op jit(solution)/shard_map/ppermute | solution.py:137
  51.9 26.2 %collective-permute-done.12 = f32[5,4,48,130]{3,2,1,0:T(8,128)} collective-permute-done((f32[5,4,48,130]{3,2,1,0:T(8,128)}, f32[5,4,48,130]{3,2,1,0:T(8,128)}, u32[]{:S(2)}, u32[]{:S(2)}) %collective-permute-start.12) | collective-permute-done | bytes 499232 | tf_op jit(solution)/shard_map/ppermute | solution.py:137
  78.0 28.6 %collective-permute-start.3 = (f32[5,4,48,1]{3,2,1,0:T(8,128)}, f32[5,4,48,1]{3,2,1,0:T(8,128)}, u32[]{:S(2)}, u32[]{:S(2)}) collective-permute-start(f32[5,4,48,1]{3,2,1,0:T(8,128)} %get-tuple-element.23), channel_id=1, source_target_pairs={{1,0},{2,1},{3,2},{4,3},{5,4},{6,5},{7,6},{8,7},{9,8},{10,9},{11,1... | collective-permute-start | bytes 11528 | tf_op jit(solution)/shard_map/ppermute | solution.py:23
  108.5 2.8 collective-permute-start.1
  111.3 2.8 collective-permute-start
  114.1 2.8 add_add_fusion
  125.0 4.7 %all-to-all-start = ((f32[8,5,4,18,130]{4,2,3,1,0:T(4,128)}), f32[8,5,4,18,130]{4,2,3,1,0:T(4,128)}, u32[]{:S(2)}, u32[]{:S(2)}) async-start(f32[8,5,4,18,130]{4,2,3,1,0:T(4,128)} %bitcast_dynamic-update-slice_fusion), calls=%async_computation | async-start | bytes 5898240 | tf_op jit(solution)/shard_map/all_to_all | solution.py:146
  135.4 29.8 %all-to-all-done = f32[8,5,4,18,130]{4,2,3,1,0:T(4,128)} async-done(((f32[8,5,4,18,130]{4,2,3,1,0:T(4,128)}), f32[8,5,4,18,130]{4,2,3,1,0:T(4,128)}, u32[]{:S(2)}, u32[]{:S(2)}) %all-to-all-start) | async-done | bytes 1497632 | tf_op jit(solution)/shard_map/all_to_all | solution.py:146
  165.2 2.5 reduce_sum.9
  169.8 3.6 %copy.41 = f32[5,4,48,128,3]{2,1,4,3,0:T(4,128)} copy(f32[5,4,48,128,3]{3,1,2,0,4:T(4,128)S(1)} %pad_maximum_fusion.8) | data formatting | bytes 2949120 | tf_op jit(solution)/shard_map/stack | solution.py:59
  173.4 3.4 %copy.42 = f32[5,4,48,384]{3,2,1,0:T(8,128)S(1)} copy(f32[5,4,48,384]{2,1,3,0:T(4,128)} %bitcast.62) | data formatting | bytes 2949120 | tf_op jit(solution)/shard_map/reshape | solution.py:63
  176.8 4.1 %multiply_add_fusion.2 = f32[5,4,48,384]{3,2,1,0:T(8,128)S(1)} fusion(f32[5,4,48,384]{3,2,1,0:T(8,128)S(1)} %copy.42, f32[5,4,48,384]{3,2,1,0:T(8,128)S(1)} %copy-done.1, f32[5,4,48,1]{3,2,1,0:T(8,128)} %collective-permute-done.3, f32[5,4,48,383]{3,2,1,0:T(8,128)} %get-tuple-element.25, f32[5,4,48,383]{3,2,1,0:T(8,128)} %get-tuple-element.24, ...), kind=kLoop, calls=%fused_computation.34 | loop fusion | flops 9584640 | bytes 11870208 | tf_op jit(solution)/shard_map/add | solution.py:157
  181.7 3.6 %collective-permute-start.16 = (f32[5,4,48,1]{3,2,1,0:T(8,128)S(1)}, f32[5,4,48,1]{3,2,1,0:T(8,128)S(1)}, u32[]{:S(2)}, u32[]{:S(2)}) collective-permute-start(f32[5,4,48,1]{3,2,1,0:T(8,128)S(1)} %get-tuple-element.15), channel_id=1, source_target_pairs={{1,0},{2,1},{3,2},{4,3},{5,4},{6,5},{7,6},{8,7},{9,8},{10,9},{11,1... | collective-permute-start | bytes 11528 | tf_op jit(solution)/shard_map/ppermute | solution.py:23
  187.3 3.1 collective-permute-start.14
  190.4 2.6 collective-permute-start.13
  195.5 4.7 %collective-permute-done.15 = f32[5,4,48,1]{3,2,1,0:T(8,128)S(1)} collective-permute-done((f32[5,4,48,1]{3,2,1,0:T(8,128)S(1)}, f32[5,4,48,1]{3,2,1,0:T(8,128)S(1)}, u32[]{:S(2)}, u32[]{:S(2)}) %collective-permute-start.15) | collective-permute-done | bytes 3872 | tf_op jit(solution)/shard_map/ppermute | solution.py:22
  202.7 5.2 %collective-permute-start.20 = (f32[5,4,48,1]{3,2,1,0:T(8,128)S(1)}, f32[5,4,48,1]{3,2,1,0:T(8,128)S(1)}, u32[]{:S(2)}, u32[]{:S(2)}) collective-permute-start(f32[5,4,48,1]{3,2,1,0:T(8,128)S(1)} %get-tuple-element.7), channel_id=1, source_target_pairs={{1,0},{2,1},{3,2},{4,3},{5,4},{6,5},{7,6},{8,7},{9,8},{10,9},{11,1... | collective-permute-start | bytes 11528 | tf_op jit(solution)/shard_map/ppermute | solution.py:23
  209.8 4.3 %collective-permute-start.18 = (f32[5,4,1,384]{3,2,1,0:T(1,128)S(1)}, f32[5,4,1,384]{3,2,1,0:T(1,128)S(1)}, u32[]{:S(2)}, u32[]{:S(2)}) collective-permute-start(f32[5,4,1,384]{3,2,1,0:T(1,128)S(1)} %get-tuple-element.3), channel_id=1, source_target_pairs={{16,0},{32,16},{48,32},{64,48},{80,64},{96,80},{112,96},{17,1},{33... | collective-permute-start | bytes 92168 | tf_op jit(solution)/shard_map/ppermute | solution.py:21
  216.5 3.7 %collective-permute-done.19 = f32[5,4,48,1]{3,2,1,0:T(8,128)S(1)} collective-permute-done((f32[5,4,48,1]{3,2,1,0:T(8,128)S(1)}, f32[5,4,48,1]{3,2,1,0:T(8,128)S(1)}, u32[]{:S(2)}, u32[]{:S(2)}) %collective-permute-start.19) | collective-permute-done | bytes 3872 | tf_op jit(solution)/shard_map/ppermute | solution.py:22
  223.1 3.5 %collective-permute-start.21 = (f32[5,4,16,128]{3,2,1,0:T(8,128)S(1)}, f32[5,4,16,128]{3,2,1,0:T(8,128)S(1)}, u32[]{:S(2)}, u32[]{:S(2)}) collective-permute-start(f32[5,4,16,128]{3,2,1,0:T(8,128)S(1)} %fusion), channel_id=1, source_target_pairs={{0,16},{16,32},{32,48},{48,64},{64,80},{80,96},{96,112},{112,0},{1... | collective-permute-start | bytes 491528 | tf_op jit(solution)/shard_map/ppermute | solution.py:164
  228.8 2.5 collective-permute-start.22
  233.5 2.5 collective-permute-start.23
  241.4 3.5 %collective-permute-start.27 = (f32[5,4,16,128]{3,2,1,0:T(8,128)S(1)}, f32[5,4,16,128]{3,2,1,0:T(8,128)S(1)}, u32[]{:S(2)}, u32[]{:S(2)}) collective-permute-start(f32[5,4,16,128]{3,2,1,0:T(8,128)S(1)} %collective-permute-done.26), channel_id=1, source_target_pairs={{0,112},{16,0},{32,16},{48,32},{64,48},{80,64},{96,80},{112,96},{1... | collective-permute-start | bytes 491528 | tf_op jit(solution)/shard_map/ppermute | solution.py:166
  249.7 6.2 %collective-permute-start.30 = (f32[5,4,48,128]{3,2,1,0:T(8,128)S(1)}, f32[5,4,48,128]{3,2,1,0:T(8,128)S(1)}, u32[]{:S(2)}, u32[]{:S(2)}) collective-permute-start(f32[5,4,48,128]{3,2,1,0:T(8,128)S(1)} %pad_dynamic-slice_fusion.13), channel_id=1, source_target_pairs={{0,8},{3,9},{6,10},{9,11},{12,12},{15,13},{16,24},{19,25},{22,26},... | collective-permute-start | bytes 1474568 | tf_op jit(solution)/shard_map/ppermute | solution.py:179
  259.2 33.2 %collective-permute-done.28 = f32[5,4,48,128]{3,2,1,0:T(8,128)S(1)} collective-permute-done((f32[5,4,48,128]{3,2,1,0:T(8,128)S(1)}, f32[5,4,48,128]{3,2,1,0:T(8,128)S(1)}, u32[]{:S(2)}, u32[]{:S(2)}) %collective-permute-start.28) | collective-permute-done | bytes 491552 | tf_op jit(solution)/shard_map/ppermute | solution.py:179
  292.6 12.5 %collective-permute-done.32 = f32[5,4,48,128]{3,2,1,0:T(8,128)S(1)} collective-permute-done((f32[5,4,48,128]{3,2,1,0:T(8,128)S(1)}, f32[5,4,48,128]{3,2,1,0:T(8,128)S(1)}, u32[]{:S(2)}, u32[]{:S(2)}) %collective-permute-start.32) | collective-permute-done | bytes 491552 | tf_op jit(solution)/shard_map/ppermute | solution.py:179
  (137 shorter events, 70.0 us)
Async XLA Ops:
  3.0 23.5 %collective-permute-start.7 = (f32[5,4,48,1]{3,2,1,0:T(8,128)}, f32[5,4,48,1]{3,2,1,0:T(8,128)}, u32[]{:S(2)}, u32[]{:S(2)}) collective-permute-start(f32[5,4,48,1]{3,2,1,0:T(8,128)} %get-tuple-element.36), channel_id=1, source_target_pairs={{1,0},{2,1},{3,2},{4,3},{5,4},{6,5},{7,6},{8,7},{9,8},{10,9},{11,1... | collective-permute-start | bytes 11528 | tf_op jit(solution)/shard_map/ppermute | solution.py:23
  5.1 21.4 %collective-permute-start.6 = (f32[5,4,48,1]{3,2,1,0:T(8,128)}, f32[5,4,48,1]{3,2,1,0:T(8,128)}, u32[]{:S(2)}, u32[]{:S(2)}) collective-permute-start(f32[5,4,48,1]{3,2,1,0:T(8,128)} %get-tuple-element.35), channel_id=1, source_target_pairs={{0,1},{1,2},{2,3},{3,4},{4,5},{5,6},{6,7},{7,8},{8,9},{9,10},{10,1... | collective-permute-start | bytes 11528 | tf_op jit(solution)/shard_map/ppermute | solution.py:22
  9.0 17.5 %collective-permute-start.5 = (f32[5,4,1,384]{3,2,1,0:T(1,128)}, f32[5,4,1,384]{3,2,1,0:T(1,128)}, u32[]{:S(2)}, u32[]{:S(2)}) collective-permute-start(f32[5,4,1,384]{3,2,1,0:T(1,128)} %get-tuple-element.32), channel_id=1, source_target_pairs={{16,0},{32,16},{48,32},{64,48},{80,64},{96,80},{112,96},{17,1},{33... | collective-permute-start | bytes 92168 | tf_op jit(solution)/shard_map/ppermute | solution.py:21
  12.1 14.4 %collective-permute-start.4 = (f32[5,4,1,384]{3,2,1,0:T(1,128)}, f32[5,4,1,384]{3,2,1,0:T(1,128)}, u32[]{:S(2)}, u32[]{:S(2)}) collective-permute-start(f32[5,4,1,384]{3,2,1,0:T(1,128)} %get-tuple-element.31), channel_id=1, source_target_pairs={{0,16},{16,32},{32,48},{48,64},{64,80},{80,96},{96,112},{1,17},{17... | collective-permute-start | bytes 92168 | tf_op jit(solution)/shard_map/ppermute | solution.py:20
  33.2 44.8 %collective-permute-start.12 = (f32[5,4,48,130]{3,2,1,0:T(8,128)}, f32[5,4,48,130]{3,2,1,0:T(8,128)}, u32[]{:S(2)}, u32[]{:S(2)}) collective-permute-start(f32[5,4,48,130]{3,2,1,0:T(8,128)} %get-tuple-element.29), channel_id=1, source_target_pairs={{9,2},{10,5},{11,8},{12,11},{13,14},{25,18},{26,21},{27,24},{28,27... | collective-permute-start | bytes 1497608 | tf_op jit(solution)/shard_map/ppermute | solution.py:137
  36.5 70.1 %collective-permute-start.11 = (f32[5,4,48,130]{3,2,1,0:T(8,128)}, f32[5,4,48,130]{3,2,1,0:T(8,128)}, u32[]{:S(2)}, u32[]{:S(2)}) collective-permute-start(f32[5,4,48,130]{3,2,1,0:T(8,128)} %get-tuple-element.28), channel_id=1, source_target_pairs={{8,2},{9,5},{10,8},{11,11},{12,14},{24,18},{25,21},{26,24},{27,27}... | collective-permute-start | bytes 1497608 | tf_op jit(solution)/shard_map/ppermute | solution.py:137
  38.7 69.8 %collective-permute-start.10 = (f32[5,4,48,130]{3,2,1,0:T(8,128)}, f32[5,4,48,130]{3,2,1,0:T(8,128)}, u32[]{:S(2)}, u32[]{:S(2)}) collective-permute-start(f32[5,4,48,130]{3,2,1,0:T(8,128)} %get-tuple-element.27), channel_id=1, source_target_pairs={{9,1},{10,4},{11,7},{12,10},{13,13},{25,17},{26,20},{27,23},{28,26... | collective-permute-start | bytes 1497608 | tf_op jit(solution)/shard_map/ppermute | solution.py:137
  41.0 70.3 %collective-permute-start.8 = (f32[5,4,48,130]{3,2,1,0:T(8,128)S(1)}, f32[5,4,48,130]{3,2,1,0:T(8,128)}, u32[]{:S(2)}, u32[]{:S(2)}) collective-permute-start(f32[5,4,48,130]{3,2,1,0:T(8,128)S(1)} %get-tuple-element.30), channel_id=1, source_target_pairs={{8,0},{9,3},{10,6},{11,9},{12,12},{13,15},{24,16},{25,19},{26,22},... | collective-permute-start | bytes 1497608 | tf_op jit(solution)/shard_map/ppermute | solution.py:137
  43.2 70.9 %collective-permute-start.9 = (f32[5,4,48,130]{3,2,1,0:T(8,128)S(1)}, f32[5,4,48,130]{3,2,1,0:T(8,128)}, u32[]{:S(2)}, u32[]{:S(2)}) collective-permute-start(f32[5,4,48,130]{3,2,1,0:T(8,128)S(1)} %get-tuple-element.26), channel_id=1, source_target_pairs={{8,1},{9,4},{10,7},{11,10},{12,13},{24,17},{25,20},{26,23},{27,26}... | collective-permute-start | bytes 1497608 | tf_op jit(solution)/shard_map/ppermute | solution.py:137
  78.0 98.8 %collective-permute-start.3 = (f32[5,4,48,1]{3,2,1,0:T(8,128)}, f32[5,4,48,1]{3,2,1,0:T(8,128)}, u32[]{:S(2)}, u32[]{:S(2)}) collective-permute-start(f32[5,4,48,1]{3,2,1,0:T(8,128)} %get-tuple-element.23), channel_id=1, source_target_pairs={{1,0},{2,1},{3,2},{4,3},{5,4},{6,5},{7,6},{8,7},{9,8},{10,9},{11,1... | collective-permute-start | bytes 11528 | tf_op jit(solution)/shard_map/ppermute | solution.py:23
  106.6 70.2 %collective-permute-start.2 = (f32[5,4,48,1]{3,2,1,0:T(8,128)}, f32[5,4,48,1]{3,2,1,0:T(8,128)}, u32[]{:S(2)}, u32[]{:S(2)}) collective-permute-start(f32[5,4,48,1]{3,2,1,0:T(8,128)} %get-tuple-element.22), channel_id=1, source_target_pairs={{0,1},{1,2},{2,3},{3,4},{4,5},{5,6},{6,7},{7,8},{8,9},{9,10},{10,1... | collective-permute-start | bytes 11528 | tf_op jit(solution)/shard_map/ppermute | solution.py:22
  108.5 68.3 %collective-permute-start.1 = (f32[5,4,1,384]{3,2,1,0:T(1,128)}, f32[5,4,1,384]{3,2,1,0:T(1,128)}, u32[]{:S(2)}, u32[]{:S(2)}) collective-permute-start(f32[5,4,1,384]{3,2,1,0:T(1,128)} %get-tuple-element.19), channel_id=1, source_target_pairs={{16,0},{32,16},{48,32},{64,48},{80,64},{96,80},{112,96},{17,1},{33... | collective-permute-start | bytes 92168 | tf_op jit(solution)/shard_map/ppermute | solution.py:21
  111.3 65.5 %collective-permute-start = (f32[5,4,1,384]{3,2,1,0:T(1,128)}, f32[5,4,1,384]{3,2,1,0:T(1,128)}, u32[]{:S(2)}, u32[]{:S(2)}) collective-permute-start(f32[5,4,1,384]{3,2,1,0:T(1,128)} %get-tuple-element.18), channel_id=1, source_target_pairs={{0,16},{16,32},{32,48},{48,64},{64,80},{80,96},{96,112},{1,17},{17... | collective-permute-start | bytes 92168 | tf_op jit(solution)/shard_map/ppermute | solution.py:20
  125.0 40.2 %all-to-all-start = ((f32[8,5,4,18,130]{4,2,3,1,0:T(4,128)}), f32[8,5,4,18,130]{4,2,3,1,0:T(4,128)}, u32[]{:S(2)}, u32[]{:S(2)}) async-start(f32[8,5,4,18,130]{4,2,3,1,0:T(4,128)} %bitcast_dynamic-update-slice_fusion), calls=%async_computation | async-start | bytes 5898240 | tf_op jit(solution)/shard_map/all_to_all | solution.py:146
  181.7 13.8 %collective-permute-start.16 = (f32[5,4,48,1]{3,2,1,0:T(8,128)S(1)}, f32[5,4,48,1]{3,2,1,0:T(8,128)S(1)}, u32[]{:S(2)}, u32[]{:S(2)}) collective-permute-start(f32[5,4,48,1]{3,2,1,0:T(8,128)S(1)} %get-tuple-element.15), channel_id=1, source_target_pairs={{1,0},{2,1},{3,2},{4,3},{5,4},{6,5},{7,6},{8,7},{9,8},{10,9},{11,1... | collective-permute-start | bytes 11528 | tf_op jit(solution)/shard_map/ppermute | solution.py:23
  185.4 14.8 %collective-permute-start.15 = (f32[5,4,48,1]{3,2,1,0:T(8,128)S(1)}, f32[5,4,48,1]{3,2,1,0:T(8,128)S(1)}, u32[]{:S(2)}, u32[]{:S(2)}) collective-permute-start(f32[5,4,48,1]{3,2,1,0:T(8,128)S(1)} %get-tuple-element.14), channel_id=1, source_target_pairs={{0,1},{1,2},{2,3},{3,4},{4,5},{5,6},{6,7},{7,8},{8,9},{9,10},{10,1... | collective-permute-start | bytes 11528 | tf_op jit(solution)/shard_map/ppermute | solution.py:22
  187.3 12.9 %collective-permute-start.14 = (f32[5,4,1,384]{3,2,1,0:T(1,128)S(1)}, f32[5,4,1,384]{3,2,1,0:T(1,128)S(1)}, u32[]{:S(2)}, u32[]{:S(2)}) collective-permute-start(f32[5,4,1,384]{3,2,1,0:T(1,128)S(1)} %get-tuple-element.11), channel_id=1, source_target_pairs={{16,0},{32,16},{48,32},{64,48},{80,64},{96,80},{112,96},{17,1},{33... | collective-permute-start | bytes 92168 | tf_op jit(solution)/shard_map/ppermute | solution.py:21
  190.4 9.8 %collective-permute-start.13 = (f32[5,4,1,384]{3,2,1,0:T(1,128)S(1)}, f32[5,4,1,384]{3,2,1,0:T(1,128)S(1)}, u32[]{:S(2)}, u32[]{:S(2)}) collective-permute-start(f32[5,4,1,384]{3,2,1,0:T(1,128)S(1)} %get-tuple-element.10), channel_id=1, source_target_pairs={{0,16},{16,32},{32,48},{48,64},{64,80},{80,96},{96,112},{1,17},{17... | collective-permute-start | bytes 92168 | tf_op jit(solution)/shard_map/ppermute | solution.py:20
  202.7 13.7 %collective-permute-start.20 = (f32[5,4,48,1]{3,2,1,0:T(8,128)S(1)}, f32[5,4,48,1]{3,2,1,0:T(8,128)S(1)}, u32[]{:S(2)}, u32[]{:S(2)}) collective-permute-start(f32[5,4,48,1]{3,2,1,0:T(8,128)S(1)} %get-tuple-element.7), channel_id=1, source_target_pairs={{1,0},{2,1},{3,2},{4,3},{5,4},{6,5},{7,6},{8,7},{9,8},{10,9},{11,1... | collective-permute-start | bytes 11528 | tf_op jit(solution)/shard_map/ppermute | solution.py:23
  207.9 12.3 %collective-permute-start.19 = (f32[5,4,48,1]{3,2,1,0:T(8,128)S(1)}, f32[5,4,48,1]{3,2,1,0:T(8,128)S(1)}, u32[]{:S(2)}, u32[]{:S(2)}) collective-permute-start(f32[5,4,48,1]{3,2,1,0:T(8,128)S(1)} %get-tuple-element.6), channel_id=1, source_target_pairs={{0,1},{1,2},{2,3},{3,4},{4,5},{5,6},{6,7},{7,8},{8,9},{9,10},{10,1... | collective-permute-start | bytes 11528 | tf_op jit(solution)/shard_map/ppermute | solution.py:22
  209.8 10.3 %collective-permute-start.18 = (f32[5,4,1,384]{3,2,1,0:T(1,128)S(1)}, f32[5,4,1,384]{3,2,1,0:T(1,128)S(1)}, u32[]{:S(2)}, u32[]{:S(2)}) collective-permute-start(f32[5,4,1,384]{3,2,1,0:T(1,128)S(1)} %get-tuple-element.3), channel_id=1, source_target_pairs={{16,0},{32,16},{48,32},{64,48},{80,64},{96,80},{112,96},{17,1},{33... | collective-permute-start | bytes 92168 | tf_op jit(solution)/shard_map/ppermute | solution.py:21
  214.1 6.1 %collective-permute-start.17 = (f32[5,4,1,384]{3,2,1,0:T(1,128)S(1)}, f32[5,4,1,384]{3,2,1,0:T(1,128)S(1)}, u32[]{:S(2)}, u32[]{:S(2)}) collective-permute-start(f32[5,4,1,384]{3,2,1,0:T(1,128)S(1)} %get-tuple-element.2), channel_id=1, source_target_pairs={{0,16},{16,32},{32,48},{48,64},{64,80},{80,96},{96,112},{1,17},{17... | collective-permute-start | bytes 92168 | tf_op jit(solution)/shard_map/ppermute | solution.py:20
  223.1 5.7 %collective-permute-start.21 = (f32[5,4,16,128]{3,2,1,0:T(8,128)S(1)}, f32[5,4,16,128]{3,2,1,0:T(8,128)S(1)}, u32[]{:S(2)}, u32[]{:S(2)}) collective-permute-start(f32[5,4,16,128]{3,2,1,0:T(8,128)S(1)} %fusion), channel_id=1, source_target_pairs={{0,16},{16,32},{32,48},{48,64},{64,80},{80,96},{96,112},{112,0},{1... | collective-permute-start | bytes 491528 | tf_op jit(solution)/shard_map/ppermute | solution.py:164
  231.3 5.0 %collective-permute-start.25 = (f32[5,4,16,128]{3,2,1,0:T(8,128)S(1)}, f32[5,4,16,128]{3,2,1,0:T(8,128)S(1)}, u32[]{:S(2)}, u32[]{:S(2)}) collective-permute-start(f32[5,4,16,128]{3,2,1,0:T(8,128)S(1)} %fusion), channel_id=1, source_target_pairs={{0,112},{16,0},{32,16},{48,32},{64,48},{80,64},{96,80},{112,96},{1... | collective-permute-start | bytes 491528 | tf_op jit(solution)/shard_map/ppermute | solution.py:166
  233.5 5.6 %collective-permute-start.23 = (f32[5,4,16,128]{3,2,1,0:T(8,128)S(1)}, f32[5,4,16,128]{3,2,1,0:T(8,128)S(1)}, u32[]{:S(2)}, u32[]{:S(2)}) collective-permute-start(f32[5,4,16,128]{3,2,1,0:T(8,128)S(1)} %collective-permute-done.22), channel_id=1, source_target_pairs={{0,16},{16,32},{32,48},{48,64},{64,80},{80,96},{96,112},{112,0},{1... | collective-permute-start | bytes 491528 | tf_op jit(solution)/shard_map/ppermute | solution.py:164
  236.3 5.1 %collective-permute-start.26 = (f32[5,4,16,128]{3,2,1,0:T(8,128)S(1)}, f32[5,4,16,128]{3,2,1,0:T(8,128)S(1)}, u32[]{:S(2)}, u32[]{:S(2)}) collective-permute-start(f32[5,4,16,128]{3,2,1,0:T(8,128)S(1)} %collective-permute-done.25), channel_id=1, source_target_pairs={{0,112},{16,0},{32,16},{48,32},{64,48},{80,64},{96,80},{112,96},{1... | collective-permute-start | bytes 491528 | tf_op jit(solution)/shard_map/ppermute | solution.py:166
  239.1 6.0 %collective-permute-start.24 = (f32[5,4,16,128]{3,2,1,0:T(8,128)S(1)}, f32[5,4,16,128]{3,2,1,0:T(8,128)S(1)}, u32[]{:S(2)}, u32[]{:S(2)}) collective-permute-start(f32[5,4,16,128]{3,2,1,0:T(8,128)S(1)} %collective-permute-done.23), channel_id=1, source_target_pairs={{0,16},{16,32},{32,48},{48,64},{64,80},{80,96},{96,112},{112,0},{1... | collective-permute-start | bytes 491528 | tf_op jit(solution)/shard_map/ppermute | solution.py:164
  246.5 45.9 %collective-permute-start.28 = (f32[5,4,48,128]{3,2,1,0:T(8,128)S(1)}, f32[5,4,48,128]{3,2,1,0:T(8,128)S(1)}, u32[]{:S(2)}, u32[]{:S(2)}) collective-permute-start(f32[5,4,48,128]{3,2,1,0:T(8,128)S(1)} %pad_dynamic-slice_fusion.13), channel_id=1, source_target_pairs={{1,9},{4,10},{7,11},{10,12},{13,13},{17,25},{20,26},{23,27},{26,28... | collective-permute-start | bytes 1474568 | tf_op jit(solution)/shard_map/ppermute | solution.py:179
  247.8 44.7 %collective-permute-start.29 = (f32[5,4,48,128]{3,2,1,0:T(8,128)S(1)}, f32[5,4,48,128]{3,2,1,0:T(8,128)S(1)}, u32[]{:S(2)}, u32[]{:S(2)}) collective-permute-start(f32[5,4,48,128]{3,2,1,0:T(8,128)S(1)} %pad_dynamic-slice_fusion.13), channel_id=1, source_target_pairs={{2,9},{5,10},{8,11},{11,12},{14,13},{18,25},{21,26},{24,27},{27,28... | collective-permute-start | bytes 1474568 | tf_op jit(solution)/shard_map/ppermute | solution.py:179
  249.7 42.8 %collective-permute-start.30 = (f32[5,4,48,128]{3,2,1,0:T(8,128)S(1)}, f32[5,4,48,128]{3,2,1,0:T(8,128)S(1)}, u32[]{:S(2)}, u32[]{:S(2)}) collective-permute-start(f32[5,4,48,128]{3,2,1,0:T(8,128)S(1)} %pad_dynamic-slice_fusion.13), channel_id=1, source_target_pairs={{0,8},{3,9},{6,10},{9,11},{12,12},{15,13},{16,24},{19,25},{22,26},... | collective-permute-start | bytes 1474568 | tf_op jit(solution)/shard_map/ppermute | solution.py:179
  256.6 36.0 %collective-permute-start.31 = (f32[5,4,48,128]{3,2,1,0:T(8,128)S(1)}, f32[5,4,48,128]{3,2,1,0:T(8,128)S(1)}, u32[]{:S(2)}, u32[]{:S(2)}) collective-permute-start(f32[5,4,48,128]{3,2,1,0:T(8,128)S(1)} %pad_dynamic-slice_fusion.13), channel_id=1, source_target_pairs={{1,8},{4,9},{7,10},{10,11},{13,12},{17,24},{20,25},{23,26},{26,27}... | collective-permute-start | bytes 1474568 | tf_op jit(solution)/shard_map/ppermute | solution.py:179
  257.9 47.2 %collective-permute-start.32 = (f32[5,4,48,128]{3,2,1,0:T(8,128)S(1)}, f32[5,4,48,128]{3,2,1,0:T(8,128)S(1)}, u32[]{:S(2)}, u32[]{:S(2)}) collective-permute-start(f32[5,4,48,128]{3,2,1,0:T(8,128)S(1)} %pad_dynamic-slice_fusion.13), channel_id=1, source_target_pairs={{2,8},{5,9},{8,10},{11,11},{14,12},{18,24},{21,25},{24,26},{27,27}... | collective-permute-start | bytes 1474568 | tf_op jit(solution)/shard_map/ppermute | solution.py:179
  (14 other events, 123.3 us)
